TPU v7x, 32 devices: a whole 2x2x4 slice. The times are simulated.
32 devices in a mesh: table: 8 (over z, core), bal: 4 (over y, x).
Axes of the slice: x: 2, y: 2, z: 4, core: 2. Of those that a mesh axis runs over, the one named last changes fastest.
Arguments:
- item_ids: int32 [8192], P(('table', 'bal')), may hold values from 0 to 8191, as said below
- hot_slot: int32 [8192], replicated, may hold values from 0 to 1024, as said below
- hot_rows: bfloat16 [1024, 512], replicated, may hold values from -6 to 6
- cold_rows: bfloat16 [8192, 512], P('table'), may hold values from -6 to 6
- hist_lengths: int32 [64], replicated, may hold values from 1 to 128
- out_grad: bfloat16 [8192, 512], P(('table', 'bal')), may hold values from -6 to 6
- w_uvqk: bfloat16 [512, 2048], replicated, may hold values from -0.25 to 0.25
- w_out: bfloat16 [512, 512], replicated, may hold values from -0.25 to 0.25
Outputs:
- layer_out: bfloat16 [8192, 512], P(('table', 'bal'))
- grad_uvqk: float32 [4096, 2048], P(('table', 'bal'))
- grad_out_proj: float32 [4096, 512], P(('table', 'bal'))
Inputs may be any that keep to these rules, and one draw needn't show every extreme that they name: `item_ids`: item i lies in table shard i // 1024. In each device's block of 256 token slots at most 32 tokens with cold items name items of one shard, and some shard gets exactly 32 of them in every block. `hot_slot`: each value below 1024 is taken by exactly one item; 1024 marks a cold item.
All inputs are finite; a program needn't handle non-finite values.
Results may differ from a plain program's by a relative error of at most 0.012.
Values may be sent and summed in bfloat16 or wider, within the bound.
No kernel may reach another device: no remote copies, remote signals or barrier semaphores. Data moves between devices by JAX's collectives and lax.ppermute only.
A program may use at most 64 MiB of HBM per device.

v0:
```python
import math

import jax
import jax.numpy as jnp
from jax import lax
from jax.sharding import PartitionSpec as P

HEADS = 4
MAXLEN = 128
TILE = 64


def norm_rows(values_in):
    average = jnp.mean(values_in, axis=-1, keepdims=True)
    centred = values_in - average
    spread = jnp.mean(centred * centred, axis=-1, keepdims=True)
    return centred * lax.rsqrt(spread + 1e-05)


def attend(hidden, length):
    row_count = hidden.shape[0]
    features = hidden.shape[1] // 4
    head_size = features // HEADS
    activated = jax.nn.silu(hidden)
    gate_part = activated[:, :features].astype(jnp.bfloat16)
    value_part = activated[:, features : 2 * features].astype(jnp.bfloat16)
    query_part = activated[:, 2 * features : 3 * features].astype(jnp.bfloat16)
    key_part = activated[:, 3 * features :].astype(jnp.bfloat16)
    query_heads = query_part.reshape(row_count, HEADS, head_size)
    key_heads = key_part.reshape(row_count, HEADS, head_size)
    value_heads = value_part.reshape(row_count, HEADS, head_size)
    scores = jnp.einsum(
        "ihe,jhe->hij", query_heads, key_heads, preferred_element_type=jnp.float32
    ) * (1.0 / math.sqrt(head_size))
    position = jnp.arange(row_count, dtype=jnp.int32)
    allowed = (position[None, :] <= position[:, None]) & (position[:, None] < length)
    weights = jnp.where(allowed[None], jax.nn.silu(scores), 0.0).astype(jnp.bfloat16)
    mixed = jnp.einsum(
        "hij,jhe->ihe", weights, value_heads, preferred_element_type=jnp.float32
    ).reshape(row_count, features)
    return (norm_rows(mixed) * gate_part.astype(jnp.float32)).astype(jnp.bfloat16)


def user_pass(user_emb, user_cot, length, w_uvqk, w_out, grad_scale):
    row_count = user_emb.shape[0]
    normed = norm_rows(user_emb.astype(jnp.float32)).astype(jnp.bfloat16)
    hidden = jnp.dot(normed, w_uvqk, preferred_element_type=jnp.float32)
    gated, pullback = jax.vjp(lambda hidden_in: attend(hidden_in, length), hidden)
    output = (
        user_emb.astype(jnp.float32) + jnp.dot(gated, w_out, preferred_element_type=jnp.float32)
    ).astype(jnp.bfloat16)
    is_valid = jnp.arange(row_count, dtype=jnp.int32) < length
    signal = (jnp.where(is_valid[:, None], user_cot.astype(jnp.float32), 0.0) * grad_scale).astype(
        jnp.bfloat16
    )
    back_signal = jnp.dot(signal, w_out.T, preferred_element_type=jnp.float32).astype(jnp.bfloat16)
    grad_hidden = pullback(back_signal)[0].astype(jnp.bfloat16)
    grad_first = jnp.einsum("td,tf->df", normed, grad_hidden, preferred_element_type=jnp.float32)
    grad_second = jnp.einsum("td,tf->df", gated, signal, preferred_element_type=jnp.float32)
    return (output, grad_first, grad_second)


def run_users(emb_stack, cot_stack, len_stack, w_uvqk, w_out, grad_scale):
    features = emb_stack.shape[2]

    def per_user(running, inputs):
        user_emb, user_cot, length = inputs

        def short_pass():
            output, grad_first, grad_second = user_pass(
                user_emb[:TILE], user_cot[:TILE], length, w_uvqk, w_out, grad_scale
            )
            return (jnp.concatenate([output, user_emb[TILE:]], axis=0), grad_first, grad_second)

        def long_pass():
            return user_pass(user_emb, user_cot, length, w_uvqk, w_out, grad_scale)

        output, grad_first, grad_second = lax.cond(length <= TILE, short_pass, long_pass)
        return ((running[0] + grad_first, running[1] + grad_second), output)

    initial = (
        jnp.zeros((features, 4 * features), jnp.float32),
        jnp.zeros((features, features), jnp.float32),
    )
    return lax.scan(per_user, initial, (emb_stack, cot_stack, len_stack))


def per_device(item_ids, hot_slot, hot_rows, cold_rows, hist_lengths, out_grad, w_uvqk, w_out):
    owners = lax.axis_size("table")
    token_count = item_ids.shape[0]
    shard_rows = cold_rows.shape[0]
    hot_count = hot_rows.shape[0]
    capacity = token_count // owners
    hot_index = jnp.take(hot_slot, item_ids)
    is_hot = hot_index < hot_count
    owner_of = item_ids // shard_rows
    shard_row = item_ids % shard_rows
    owner_marks = (
        (owner_of[:, None] == jnp.arange(owners, dtype=jnp.int32)[None, :])
        & jnp.logical_not(is_hot)[:, None]
    ).astype(jnp.int32)
    earlier = jnp.cumsum(owner_marks, axis=0) - owner_marks
    position = jnp.sum(earlier * owner_marks, axis=1)
    target = jnp.where(is_hot, owners, owner_of)
    requests = (
        jnp.zeros((owners, capacity), jnp.int32).at[target, position].set(shard_row, mode="drop")
    )
    found_rows = jnp.take(
        cold_rows,
        lax.all_to_all(requests, "table", split_axis=0, concat_axis=0, tiled=True),
        axis=0,
    )
    replies = lax.all_to_all(found_rows, "table", split_axis=0, concat_axis=0, tiled=True)
    cold_part = replies[owner_of, jnp.minimum(position, capacity - 1)]
    hot_part = jnp.take(hot_rows, jnp.minimum(hot_index, hot_count - 1), axis=0)
    embedded = jnp.where(is_hot[:, None], hot_part, cold_part)
    seq_len = MAXLEN
    user_count = token_count // seq_len
    features = embedded.shape[1]
    bal_count = lax.axis_size("bal")
    bal_index = lax.axis_index("bal")
    user_start = (lax.axis_index("table") * bal_count + bal_index) * user_count
    grad_scale = 1.0 / math.sqrt(bal_count * token_count)
    own_lengths = lax.dynamic_slice_in_dim(hist_lengths, user_start, user_count)
    own_emb = embedded.reshape(user_count, seq_len, features)
    own_cot = out_grad.reshape(user_count, seq_len, features)
    totals, outputs = run_users(own_emb, own_cot, own_lengths, w_uvqk, w_out, grad_scale)
    layer_out = outputs.reshape(token_count, features)
    grad_first, grad_second = (
        lax.psum_scatter(totals[0], "bal", scatter_dimension=0, tiled=True),
        lax.psum_scatter(totals[1], "bal", scatter_dimension=0, tiled=True),
    )
    return (layer_out, grad_first, grad_second)


def solution(mesh):
    return jax.shard_map(
        per_device,
        mesh=mesh,
        in_specs=(
            P(("table", "bal")),
            P(),
            P(),
            P("table", None),
            P(),
            P(("table", "bal"), None),
            P(),
            P(),
        ),
        out_specs=(P(("table", "bal"), None), P(("table", "bal"), None), P(("table", "bal"), None)),
        check_vma=False,
    )
```

profile of v0, /device:TPU:0, one launch (start us, length us, event | category | flops | bytes accessed | tf_op | source)
XLA Modules:
  0.0 192.8 jit_solution(8728993358723699152)
XLA Ops:
  7.2 0.8 and_select_fusion
  8.0 2.0 %gather_fusion = s32[256]{0:T(256)S(1)} fusion(s32[8192]{0:T(1024)} %param.13, s32[1024]{0:T(1024)S(1)} %pad_clamp_fusion.2), kind=kCustom, calls=%fused_computation | custom fusion | bytes 3072 | tf_op jit(solution)/shard_map/jit(_take)/gather | solution.py:94
  10.0 0.7 and_bitcast_fusion
  11.8 11.2 %scatter_fusion = s32[8,32]{1,0:T(8,128)S(1)} fusion(s32[8,32]{1,0:T(8,128)S(1)} %broadcast_in_dim.170, s32[256]{0:T(256)S(1)} %bitcast.181, s32[256]{0:T(256)S(1)} %get-tuple-element.184), kind=kCustom, calls=%fused_computation.4 | custom fusion | bytes 5120 | tf_op jit(solution)/shard_map/scatter | solution.py:106
  23.0 11.7 %all_to_all.20 = s32[8,1,32]{2,1,0:T(1,128)S(1)} all-to-all(s32[8,1,32]{2,1,0:T(1,128)S(1)} %bitcast.174), channel_id=1, replica_groups=mesh['table'=8,'bal'=4] {'table'}, dimensions={0} | all-to-all | bytes 2048 | tf_op jit(solution)/shard_map/all_to_all | solution.py:110
  34.8 1.2 gather_fusion.2
  36.0 0.8 broadcast_select_fusion
  36.8 3.4 %all-to-all-start.1 = ((bf16[8,32,512]{2,1,0:T(8,128)(2,1)}), bf16[8,32,512]{2,1,0:T(8,128)(2,1)S(1)}, u32[]{:S(2)}, u32[]{:S(2)}) async-start(bf16[8,32,512]{2,1,0:T(8,128)(2,1)} %broadcast_select_fusion), calls=%async_computation.1 | async-start | bytes 524288 | tf_op jit(solution)/shard_map/all_to_all | solution.py:113
  40.5 1.2 gather_fusion.1
  41.7 8.1 %all-to-all-done.1 = bf16[8,32,512]{2,1,0:T(8,128)(2,1)S(1)} async-done(((bf16[8,32,512]{2,1,0:T(8,128)(2,1)}), bf16[8,32,512]{2,1,0:T(8,128)(2,1)S(1)}, u32[]{:S(2)}, u32[]{:S(2)}) %all-to-all-start.1) | async-done | bytes 262176 | tf_op jit(solution)/shard_map/all_to_all | solution.py:113
  49.8 2.1 %gather_fusion.3 = bf16[256,512]{1,0:T(8,128)(2,1)S(1)} fusion(bf16[8,32,512]{2,1,0:T(8,128)(2,1)S(1)} %all-to-all-done.1, s32[256]{0:T(256)S(1)} %bitcast.180), kind=kCustom, calls=%fused_computation.3 | custom fusion | bytes 526336 | tf_op jit(solution)/shard_map/gather | solution.py:114
  51.9 0.8 select_select_fusion
  52.8 50.8 %while.15 = (s32[]{:T(128)}, f32[512,2048]{1,0:T(8,128)}, f32[512,512]{1,0:T(8,128)}, bf16[2,128,512]{2,1,0:T(8,128)(2,1)}, s32[2]{0:T(128)S(1)}, /*index=5*/bf1...) while((s32[]{:T(128)}, f32[512,2048]{1,0:T(8,128)}, ...), condition=%wide.region_19.20_spmd.clone, body=%wide.region_4.19_spmd.clone.sunk | while | flops 852329344 | bytes 48458384 | solution.py:85
  52.8 1.0 dynamic-slice_bitcast_fusion.3
  55.1 14.8 %conditional.3 = (f32[512,2048]{1,0:T(8,128)}, f32[512,512]{1,0:T(8,128)S(1)}, bf16[1,128,512]{2,1,0:T(8,128)(2,1)S(1)}) conditional(s32[]{:T(128)} %convert_element_type.322, (bf16[128,512]{1,0:T(8,128)(2,1)S(1)}, s32[]{:T(128)}, bf16[128,512]{1,0:T(8,128)(2,1)S(1)}, bf16[512,512]{1,0:T(8,128)(2,1)S(1)}, bf16[512,2048]{1,0:T(8,128)(2,1)}) %tuple.81, ...), branch_computations={%region_5.11_spmd, %region_12.18_spmd} | conditional | flops 849707904 | bytes 21457120 | solution.py:78
  55.5 3.1 %multiply_convert_fusion = (bf16[128,2048]{1,0:T(8,128)(2,1)S(1)}, f32[128,2048]{1,0:T(8,128)}) fusion(bf16[512,2048]{1,0:T(8,128)(2,1)} %get-tuple-element.61, bf16[128,512]{1,0:T(8,128)(2,1)S(1)} %get-tuple-element.57, f32[128]{0:T(128)S(1)} %add_rsqrt_fusion, f32[128]{0:T(128)S(1)} %broadcast_multiply_fusion.1), kind=kOutput, calls=%fused_computation.21 | convolution fusion | flops 270008320 | bytes 3802112 | tf_op jit(solution)/shard_map/while/body/eval_jaxpr/cond/branch_0_fun/dot_general | solution.py:47
  61.1 1.1 multiply_reduce_fusion
  62.8 0.9 fusion.107
  65.3 4.1 %fusion.8 = f32[512,2048]{1,0:T(8,128)} fusion(f32[128,2048]{1,0:T(8,128)} %get-tuple-element.158, bf16[128,512]{1,0:T(8,128)(2,1)S(1)} %get-tuple-element.151, bf16[128,512]{1,0:T(8,128)(2,1)S(1)} %copy.94, bf16[128,512]{1,0:T(8,128)(2,1)S(1)} %copy.93, bf16[128,512]{1,0:T(8,128)(2,1)S(1)} %copy.92, bf16[128,512]{1,0:T(8,128)(2,1)S(1)} %get-tuple-element.57, ...), kind=kOutput, calls=%fused_computation.23 | convolution fusion | flops 273154048 | bytes 5899264 | tf_op jit(solution)/shard_map/while/body/eval_jaxpr/cond/branch_0_fun/td,tf->df/dot_general | solution.py:58
  70.0 5.4 %select_add_fusion.4 = f32[512,2048]{1,0:T(8,128)} fusion(f32[512,2048]{1,0:T(8,128)} %get-tuple-element.250, f32[512,2048]{1,0:T(8,128)} %get-tuple-element.272, pred[]{:T(512)S(6)} %compare.20), kind=kLoop, calls=%fused_computation.167.clone.1 | loop fusion | flops 2097152 | bytes 12582913 | tf_op jit(solution)/shard_map/while/body/eval_jaxpr/add | solution.py:79
  75.8 1.1 copy-done.3
  77.6 1.0 dynamic-slice_bitcast_fusion.3
  79.9 14.8 %conditional.3 = (f32[512,2048]{1,0:T(8,128)}, f32[512,512]{1,0:T(8,128)S(1)}, bf16[1,128,512]{2,1,0:T(8,128)(2,1)S(1)}) conditional(s32[]{:T(128)} %convert_element_type.322, (bf16[128,512]{1,0:T(8,128)(2,1)S(1)}, s32[]{:T(128)}, bf16[128,512]{1,0:T(8,128)(2,1)S(1)}, bf16[512,512]{1,0:T(8,128)(2,1)S(1)}, bf16[512,2048]{1,0:T(8,128)(2,1)}) %tuple.81, ...), branch_computations={%region_5.11_spmd, %region_12.18_spmd} | conditional | flops 849707904 | bytes 21457120 | solution.py:78
  80.3 3.1 %multiply_convert_fusion = (bf16[128,2048]{1,0:T(8,128)(2,1)S(1)}, f32[128,2048]{1,0:T(8,128)}) fusion(bf16[512,2048]{1,0:T(8,128)(2,1)} %get-tuple-element.61, bf16[128,512]{1,0:T(8,128)(2,1)S(1)} %get-tuple-element.57, f32[128]{0:T(128)S(1)} %add_rsqrt_fusion, f32[128]{0:T(128)S(1)} %broadcast_multiply_fusion.1), kind=kOutput, calls=%fused_computation.21 | convolution fusion | flops 270008320 | bytes 3802112 | tf_op jit(solution)/shard_map/while/body/eval_jaxpr/cond/branch_0_fun/dot_general | solution.py:47
  85.9 1.1 multiply_reduce_fusion
  87.6 0.9 fusion.107
  90.1 4.1 %fusion.8 = f32[512,2048]{1,0:T(8,128)} fusion(f32[128,2048]{1,0:T(8,128)} %get-tuple-element.158, bf16[128,512]{1,0:T(8,128)(2,1)S(1)} %get-tuple-element.151, bf16[128,512]{1,0:T(8,128)(2,1)S(1)} %copy.94, bf16[128,512]{1,0:T(8,128)(2,1)S(1)} %copy.93, bf16[128,512]{1,0:T(8,128)(2,1)S(1)} %copy.92, bf16[128,512]{1,0:T(8,128)(2,1)S(1)} %get-tuple-element.57, ...), kind=kOutput, calls=%fused_computation.23 | convolution fusion | flops 273154048 | bytes 5899264 | tf_op jit(solution)/shard_map/while/body/eval_jaxpr/cond/branch_0_fun/td,tf->df/dot_general | solution.py:58
  94.8 6.7 %select_add_fusion.4 = f32[512,2048]{1,0:T(8,128)} fusion(f32[512,2048]{1,0:T(8,128)} %get-tuple-element.250, f32[512,2048]{1,0:T(8,128)} %get-tuple-element.272, pred[]{:T(512)S(6)} %compare.20), kind=kLoop, calls=%fused_computation.167.clone.1 | loop fusion | flops 2097152 | bytes 12582913 | tf_op jit(solution)/shard_map/while/body/eval_jaxpr/add | solution.py:79
  101.8 1.1 copy-done.3
  103.7 0.7 reduce-scatter.3.cloned.1.call-update
  104.4 25.3 %reduce-scatter.5.cloned.1.call-done = f32[128,512]{1,0:T(8,128)} async-done(((f32[512,512]{1,0:T(8,128)}), f32[128,512]{1,0:T(8,128)}) %reduce-scatter.5.cloned.1.call-update) | async-done | bytes 262160 | tf_op jit(solution)/shard_map/reduce_scatter | solution.py:131
  129.7 56.2 %reduce-scatter.3.cloned.1.call-done = f32[128,2048]{1,0:T(8,128)} async-done(((f32[512,2048]{1,0:T(8,128)}), f32[128,2048]{1,0:T(8,128)}) %reduce-scatter.3.cloned.1.call-update) | async-done | bytes 1048592 | tf_op jit(solution)/shard_map/reduce_scatter | solution.py:130
  (141 shorter events, 15.8 us)
Async XLA Ops:
  7.2 27.6 %copy-start = (bf16[1024,512]{1,0:T(8,128)(2,1)S(1)}, bf16[1024,512]{1,0:T(8,128)(2,1)}, u32[]{:S(2)}) copy-start(bf16[1024,512]{1,0:T(8,128)(2,1)} %param.15) | copy-start | bytes 3145732
  7.2 33.3 %copy-start.4 = (bf16[1024,512]{1,0:T(8,128)(2,1)S(1)}, bf16[1024,512]{1,0:T(8,128)(2,1)}, u32[]{:S(2)}) copy-start(bf16[1024,512]{1,0:T(8,128)(2,1)} %param.14) | copy-start | bytes 3145732
  10.0 31.6 %copy-start.12 = (s32[64]{0:T(128)S(1)}, s32[64]{0:T(128)}, u32[]{:S(2)}) copy-start(s32[64]{0:T(128)} %param.16) | copy-start | bytes 772
  34.8 18.0 %copy-start.1 = (bf16[512,512]{1,0:T(8,128)(2,1)S(1)}, bf16[512,512]{1,0:T(8,128)(2,1)}, u32[]{:S(2)}) copy-start(bf16[512,512]{1,0:T(8,128)(2,1)} %param.19) | copy-start | bytes 1572868
  36.8 13.1 %all-to-all-start.1 = ((bf16[8,32,512]{2,1,0:T(8,128)(2,1)}), bf16[8,32,512]{2,1,0:T(8,128)(2,1)S(1)}, u32[]{:S(2)}, u32[]{:S(2)}) async-start(bf16[8,32,512]{2,1,0:T(8,128)(2,1)} %broadcast_select_fusion), calls=%async_computation.1 | async-start | bytes 524288 | tf_op jit(solution)/shard_map/all_to_all | solution.py:113
  40.2 89.5 %reduce-scatter.5.cloned.1.call-start = ((), (), s32[]{:S(2)}) async-start(), calls=%async_computation.5 | async-start | bytes 1310720 | tf_op jit(solution)/shard_map/reduce_scatter | solution.py:131
  52.8 2.3 %copy-start.13 = (s32[2]{0:T(128)}, s32[2]{0:T(128)S(1)}, u32[]{:S(2)}) copy-start(s32[2]{0:T(128)S(1)} %get-tuple-element.287) | copy-start | bytes 28 | tf_op jit(solution)/shard_map/while
  55.3 3.3 %copy-start.8 = (f32[128]{0:T(128)}, f32[128]{0:T(128)S(1)}, u32[]{:S(2)}) copy-start(f32[128]{0:T(128)S(1)} %broadcast_multiply_fusion.1) | copy-start | bytes 1540 | tf_op jit(solution)/shard_map/while/body/eval_jaxpr/cond
  55.5 3.6 %copy-start.15 = (f32[128]{0:T(128)}, f32[128]{0:T(128)S(1)}, u32[]{:S(2)}) copy-start(f32[128]{0:T(128)S(1)} %add_rsqrt_fusion) | copy-start | bytes 1540 | tf_op jit(solution)/shard_map/while/body/eval_jaxpr/cond
  60.4 0.6 copy-start.5
  63.7 1.5 copy-start.9
  63.7 1.5 copy-start.16
  65.1 4.2 %copy-start.7 = (pred[128]{0:T(512)(128)(4,1)S(1)}, pred[128]{0:T(512)(128)(4,1)}, u32[]{:S(2)}) copy-start(pred[128]{0:T(512)(128)(4,1)} %copy-done.6) | copy-start | bytes 388 | tf_op jit(solution)/shard_map/while/body/eval_jaxpr/cond
  70.0 5.5 %copy-start.2 = (f32[512,512]{1,0:T(8,128)S(1)}, f32[512,512]{1,0:T(8,128)}, u32[]{:S(2)}) copy-start(f32[512,512]{1,0:T(8,128)} %get-tuple-element.273) | copy-start | bytes 3145732 | tf_op jit(solution)/shard_map/while
  70.0 6.9 %copy-start.10 = (bf16[2,128,512]{2,1,0:T(8,128)(2,1)S(1)}, bf16[2,128,512]{2,1,0:T(8,128)(2,1)}, u32[]{:S(2)}) copy-start(bf16[2,128,512]{2,1,0:T(8,128)(2,1)} %get-tuple-element.274) | copy-start | bytes 786436 | tf_op jit(solution)/shard_map/while
  70.0 7.6 %copy-start.14 = (s32[2]{0:T(128)S(1)}, s32[2]{0:T(128)}, u32[]{:S(2)}) copy-start(s32[2]{0:T(128)} %copy-done.13) | copy-start | bytes 28 | tf_op jit(solution)/shard_map/while
  75.8 1.1 copy-start.3
  76.9 0.7 copy-start.11
  77.6 2.3 %copy-start.13 = (s32[2]{0:T(128)}, s32[2]{0:T(128)S(1)}, u32[]{:S(2)}) copy-start(s32[2]{0:T(128)S(1)} %get-tuple-element.287) | copy-start | bytes 28 | tf_op jit(solution)/shard_map/while
  80.1 3.3 %copy-start.8 = (f32[128]{0:T(128)}, f32[128]{0:T(128)S(1)}, u32[]{:S(2)}) copy-start(f32[128]{0:T(128)S(1)} %broadcast_multiply_fusion.1) | copy-start | bytes 1540 | tf_op jit(solution)/shard_map/while/body/eval_jaxpr/cond
  80.3 3.6 %copy-start.15 = (f32[128]{0:T(128)}, f32[128]{0:T(128)S(1)}, u32[]{:S(2)}) copy-start(f32[128]{0:T(128)S(1)} %add_rsqrt_fusion) | copy-start | bytes 1540 | tf_op jit(solution)/shard_map/while/body/eval_jaxpr/cond
  84.6 0.6 copy-start.6
  85.2 0.6 copy-start.5
  88.5 1.5 copy-start.9
  88.5 1.5 copy-start.16
  89.9 4.2 %copy-start.7 = (pred[128]{0:T(512)(128)(4,1)S(1)}, pred[128]{0:T(512)(128)(4,1)}, u32[]{:S(2)}) copy-start(pred[128]{0:T(512)(128)(4,1)} %copy-done.6) | copy-start | bytes 388 | tf_op jit(solution)/shard_map/while/body/eval_jaxpr/cond
  94.7 6.7 %copy-start.2 = (f32[512,512]{1,0:T(8,128)S(1)}, f32[512,512]{1,0:T(8,128)}, u32[]{:S(2)}) copy-start(f32[512,512]{1,0:T(8,128)} %get-tuple-element.273) | copy-start | bytes 3145732 | tf_op jit(solution)/shard_map/while
  94.8 8.1 %copy-start.10 = (bf16[2,128,512]{2,1,0:T(8,128)(2,1)S(1)}, bf16[2,128,512]{2,1,0:T(8,128)(2,1)}, u32[]{:S(2)}) copy-start(bf16[2,128,512]{2,1,0:T(8,128)(2,1)} %get-tuple-element.274) | copy-start | bytes 786436 | tf_op jit(solution)/shard_map/while
  94.8 8.9 %copy-start.14 = (s32[2]{0:T(128)S(1)}, s32[2]{0:T(128)}, u32[]{:S(2)}) copy-start(s32[2]{0:T(128)} %copy-done.13) | copy-start | bytes 28 | tf_op jit(solution)/shard_map/while
  101.8 1.1 copy-start.3
  102.9 0.7 copy-start.11
  103.6 82.3 %reduce-scatter.3.cloned.1.call-start = ((), (), s32[]{:S(2)}) async-start(), calls=%async_computation.4 | async-start | bytes 5242880 | tf_op jit(solution)/shard_map/reduce_scatter | solution.py:130
  (1 other events, 0.6 us)
Sparse Core Ops, SparseCore 0:
  103.8 25.8 reduce-scatter.4
  133.3 52.6 reduce-scatter.2
where the time goes:
time: 193 us
  waiting for transfers between devices  90.3 us (47%)
  local copies, waits for them, and re-layouts  27 us (14%)
  other arithmetic  23.4 us (12%)
  matrix products  20.4 us (11%)
  between operations  14.2 us (7%)
  blocking collectives  11.7 us (6%)
  starting transfers between devices  3.67 us (2%)
  loops' own time  2 us (1%)
    reduce_scatter x1, waiting for transfers between devices, per_device(): lax.psum_scatter(totals[0], 'bal', scatter_dimension=0, tiled=True)  56.2 us
    reduce_scatter x1, waiting for transfers between devices, per_device(): lax.psum_scatter(totals[1], 'bal', scatter_dimension=0, tiled=True)  25.3 us
    add x4, other arithmetic, per_user(): return ((running[0] + grad_first, running[1] + grad_second), output)  12.8 us
    all_to_all x1, blocking collectives, per_device(): lax.all_to_all(requests, 'table', split_axis=0, concat_axis=0, tiled=True)  11.7 us
    scatter x1, local copies, waits for them, and re-layouts, per_device(): jnp.zeros((owners, capacity), jnp.int32).at[target, position]  11.2 us
    dot_general x2, matrix products, user_pass(): jnp.einsum('td,tf->df', normed, grad_hidden, preferred_element_type=jnp.f...  8.14 us
    all_to_all x1, waiting for transfers between devices, per_device(): lax.all_to_all(found_rows, 'table', split_axis=0, concat_axis=0, tiled=True)  8.1 us
    dot_general x2, matrix products, user_pass(): hidden = jnp.dot(normed, w_uvqk, preferred_element_type=jnp.float32)  6.18 us
  transfers between devices with their start and end apart: 3, of which 3 were waited for; matrix products, arithmetic and copies ran while one was open for 1% of the time, Pallas kernels for 0%

commit v1 on v0

v1 whole, which is shorter than its diff:
```python
import functools
import math

import jax
import jax.numpy as jnp
from jax import lax
from jax.experimental import pallas as pl
from jax.experimental.pallas import tpu as pltpu
from jax.sharding import PartitionSpec as P

HEADS = 4
MAXLEN = 128
LANES = 128
F32 = jnp.float32
BF16 = jnp.bfloat16


def dot_nn(a, b):
    return lax.dot_general(a, b, (((1,), (0,)), ((), ())), preferred_element_type=F32)


def dot_nt(a, b):
    return lax.dot_general(a, b, (((1,), (1,)), ((), ())), preferred_element_type=F32)


def dot_tn(a, b):
    return lax.dot_general(a, b, (((0,), (0,)), ((), ())), preferred_element_type=F32)


def iota(shape, dim):
    return lax.broadcasted_iota(jnp.int32, shape, dim)


def sigmoid(x):
    return 0.5 + 0.5 * jnp.tanh(0.5 * x)


def norm_rows(x):
    centred = x - jnp.mean(x, axis=-1, keepdims=True)
    return centred * lax.rsqrt(jnp.mean(centred * centred, axis=-1, keepdims=True) + 1e-05)


def before_matrix(count):
    return (iota((count, count), 0) < iota((count, count), 1)).astype(BF16)


def table_lookup(table, ids):
    tokens = ids.shape[1]
    high = (iota((table.shape[0], tokens), 0) == ids // LANES).astype(BF16)
    lines = dot_tn(table, high)
    return jnp.sum(jnp.where(iota(lines.shape, 0) == ids % LANES, lines, 0.0), axis=0, keepdims=True)


def serve_kernel(hot_count, ids_ref, hot_ref, cold_ref, out_ref):
    sources, _, tokens = ids_ref.shape
    shard_rows = cold_ref.shape[0]
    capacity = out_ref.shape[0] // sources
    first = lax.axis_index("table") * shard_rows
    cold_table = (hot_ref[...] >= hot_count).astype(F32).astype(BF16)
    before = before_matrix(tokens)
    group = math.gcd(sources, 8)

    def serve(start):
        local, marks = [], []
        for s in range(group):
            ids = ids_ref[start + s]
            row = ids - first
            mine = (row >= 0) & (row < shard_rows)
            marks.append(jnp.where(mine, table_lookup(cold_table, ids), 0.0))
            local.append(row.astype(F32))
        mark = jnp.concatenate(marks, axis=0)
        rank = dot_nn(mark.astype(BF16), before)
        picks = []
        for s in range(group):
            chosen = (iota((capacity, tokens), 0).astype(F32) == rank[s : s + 1]) & (marks[s] > 0.5)
            wanted = jnp.sum(jnp.where(chosen, local[s], 0.0), axis=1, keepdims=True)
            picks.append((iota((capacity, shard_rows), 1).astype(F32) == wanted).astype(F32))
        pick = jnp.concatenate(picks, axis=0).astype(BF16)
        return dot_nn(pick, cold_ref[...]).astype(BF16)

    if sources == group:
        out_ref[...] = serve(0)
    else:
        span = group * capacity

        def step(i, carry):
            out_ref[pl.ds(pl.multiple_of(i * span, span), span), :] = serve(i * group)
            return carry

        lax.fori_loop(0, sources // group, step, 0)


def own_kernel(shard_rows, scale, len_ref, ids_ref, hot_ref, hot_rows_ref, cot_ref, w_out_ref,
               emb_ref, pick_ref, signal_ref, back_ref):
    tokens = ids_ref.shape[1]
    hot_count = hot_rows_ref.shape[0]
    sources = lax.axis_size("table")
    capacity = tokens // sources
    ids = ids_ref[...]
    table = hot_ref[...]
    high = table_lookup((table // 256).astype(F32).astype(BF16), ids)
    low = table_lookup((table % 256).astype(F32).astype(BF16), ids)
    hot_index = high * 256.0 + low
    cold = hot_index >= hot_count
    row = ids - iota((sources, tokens), 0) * shard_rows
    mark = jnp.where((row >= 0) & (row < shard_rows) & cold, 1.0, 0.0)
    rank = dot_nn(mark.astype(BF16), before_matrix(tokens))
    place = rank + (iota((sources, tokens), 0) * capacity).astype(F32)
    slot = jnp.sum(mark * place, axis=0, keepdims=True) - jnp.where(cold, 0.0, 1.0)
    stacked = jnp.concatenate([slot, hot_index, jnp.zeros((6, tokens), F32)], axis=0)
    columns = jnp.transpose(stacked)
    pick_ref[...] = (
        (iota((tokens, tokens), 1).astype(F32) == columns[:, 0:1]).astype(F32).astype(BF16)
    )
    hot_pick = (iota((tokens, hot_count), 1).astype(F32) == columns[:, 1:2]).astype(F32).astype(BF16)
    emb_ref[...] = dot_nn(hot_pick, hot_rows_ref[...]).astype(BF16)
    users = tokens // MAXLEN
    first_user = (lax.axis_index("table") * lax.axis_size("bal") + lax.axis_index("bal")) * users
    for u in range(users):
        rows = slice(u * MAXLEN, (u + 1) * MAXLEN)
        valid = iota((MAXLEN, 1), 0) < len_ref[first_user + u]
        signal_ref[rows, :] = (jnp.where(valid, cot_ref[rows, :].astype(F32), 0.0) * scale).astype(BF16)
    back_ref[...] = dot_nt(signal_ref[...], w_out_ref[...]).astype(BF16)


def layer_kernel(len_ref, emb_ref, pick_ref, replies_ref, signal_ref, back_ref, w_ref, w_out_ref,
                 out_ref, *rest):
    pieces = rest[:4]
    normed_t, gated_t, grad, gated, slope = rest[4:]
    tokens, features = emb_ref.shape
    head = features // HEADS
    users = tokens // MAXLEN
    bal = lax.axis_size("bal")
    me = lax.axis_index("bal")
    first_user = (lax.axis_index("table") * bal + me) * users
    inv = 1.0 / math.sqrt(head)

    emb = dot_nn(pick_ref[...], replies_ref[...]) + emb_ref[...].astype(F32)
    normed = norm_rows(emb)
    normed_t[...] = jnp.transpose(normed).astype(BF16)
    normed = normed.astype(BF16)

    def part(index):
        hidden = dot_nn(normed, w_ref[:, index * features : (index + 1) * features])
        gate = sigmoid(hidden)
        act = hidden * gate
        slope[:, index * features : (index + 1) * features] = gate * (1.0 + hidden - act)
        return act.astype(BF16)

    gate_part, value_part, query_part, key_part = (part(i) for i in range(4))
    for u in range(users):
        rows = slice(u * MAXLEN, (u + 1) * MAXLEN)
        length = len_ref[first_user + u]
        at = iota((MAXLEN, MAXLEN), 0)
        allowed = (iota((MAXLEN, MAXLEN), 1) <= at) & (at < length)
        weights, slopes, mixes = [], [], []
        for h in range(HEADS):
            cols = slice(h * head, (h + 1) * head)
            score = dot_nt(query_part[rows, cols], key_part[rows, cols]) * inv
            s = sigmoid(score)
            a = score * s
            weight = jnp.where(allowed, a, 0.0).astype(BF16)
            weights.append(weight)
            slopes.append(jnp.where(allowed, s * (1.0 + score - a) * inv, 0.0))
            mixes.append(dot_nn(weight, value_part[rows, cols]))
        mixed = jnp.concatenate(mixes, axis=1)
        centred = mixed - jnp.mean(mixed, axis=-1, keepdims=True)
        rstd = lax.rsqrt(jnp.mean(centred * centred, axis=-1, keepdims=True) + 1e-05)
        unit = centred * rstd
        gate = gate_part[rows].astype(F32)
        gated[rows, :] = (unit * gate).astype(BF16)
        back = back_ref[rows, :].astype(F32)
        d_gate = (back * unit).astype(BF16).astype(F32)
        grad[rows, 0:features] = (d_gate * slope[rows, 0:features]).astype(BF16)
        d_unit = back * gate
        d_mixed = rstd * (
            d_unit
            - jnp.mean(d_unit, axis=-1, keepdims=True)
            - unit * jnp.mean(d_unit * unit, axis=-1, keepdims=True)
        )
        d_mixed = d_mixed.astype(BF16)
        for h in range(HEADS):
            cols = slice(h * head, (h + 1) * head)
            d_mix = d_mixed[:, cols]
            d_weight = dot_nt(d_mix, value_part[rows, cols]).astype(BF16).astype(F32)
            d_score = (d_weight * slopes[h]).astype(BF16)
            d_value = dot_tn(weights[h], d_mix)
            d_query = dot_nn(d_score, key_part[rows, cols])
            d_key = dot_tn(d_score, query_part[rows, cols])
            for index, value in ((1, d_value), (2, d_query), (3, d_key)):
                where = slice(index * features + h * head, index * features + (h + 1) * head)
                grad[rows, where] = (value.astype(BF16).astype(F32) * slope[rows, where]).astype(BF16)
    out_ref[...] = (emb + dot_nn(gated[...], w_out_ref[...])).astype(BF16)
    gated_t[...] = jnp.transpose(gated[...].astype(F32)).astype(BF16)

    block = features // bal
    width = pieces[0].shape[-1]
    total = grad.shape[1]
    low, high = bal // 2, 1
    for r in range(bal):
        start = pl.multiple_of((r ^ me) * block, block)
        left = normed_t[pl.ds(start, block), :]
        first_order, second_order = split_index(r, bal)
        target, index = (pieces[0], pieces[1])[first_order[0]], first_order[1]
        target[index] = dot_nn(left, grad[:, 0:width]).astype(BF16)
        target, index = (pieces[2], pieces[3])[second_order[0]], second_order[1]
        target[index, :, 0 : total - width] = dot_nn(left, grad[:, width:total]).astype(BF16)
        out_left = gated_t[pl.ds(start, block), :]
        target[index, :, total - width : width] = dot_nn(out_left, signal_ref[...]).astype(BF16)


def bit_orders(count):
    bits = [1 << k for k in range(count.bit_length() - 1)]
    half = len(bits) // 2
    return bits, bits[half:] + bits[:half]


def split_index(r, count):
    answers = []
    for order in bit_orders(count):
        bit = order[0]
        same = [k for k in range(count) if (k & bit) == (r & bit)]
        answers.append((0 if r & bit else 1, same.index(r)))
    return answers


def halve(send, keep, order, count):
    members = [k for k in range(count) if not k & order[0]]
    for step, bit in enumerate(order):
        got = lax.ppermute(send, "bal", [(i, i ^ bit) for i in range(count)])
        total = got.astype(F32) + keep.astype(F32)
        if step + 1 == len(order):
            return total[0]
        following = order[step + 1]
        pick = lambda on: [i for i, k in enumerate(members) if bool(k & following) == on]
        send = jnp.stack([total[i] for i in pick(True)]).astype(BF16)
        keep = jnp.stack([total[i] for i in pick(False)])
        members = [k for k in members if not k & following]


def per_device(item_ids, hot_slot, hot_rows, cold_rows, hist_lengths, out_grad, w_uvqk, w_out):
    owners = lax.axis_size("table")
    bal = lax.axis_size("bal")
    tokens = item_ids.shape[0]
    features = hot_rows.shape[1]
    hot_count = hot_rows.shape[0]
    shard_rows = cold_rows.shape[0]
    hidden = w_uvqk.shape[1]
    vmem = pl.BlockSpec(memory_space=pltpu.VMEM)
    smem = pl.BlockSpec(memory_space=pltpu.SMEM)
    hot_table = hot_slot.reshape(-1, LANES)

    everyone = jnp.broadcast_to(item_ids.reshape(1, 1, tokens), (owners, 1, tokens))
    asked = lax.all_to_all(everyone, "table", split_axis=0, concat_axis=0, tiled=True)
    found = pl.pallas_call(
        functools.partial(serve_kernel, hot_count),
        out_shape=jax.ShapeDtypeStruct((tokens, features), BF16),
        in_specs=[vmem] * 3,
        out_specs=vmem,
        name="serve",
    )(asked, hot_table, cold_rows)
    replies = lax.all_to_all(found, "table", split_axis=0, concat_axis=0, tiled=True)

    wide = jax.ShapeDtypeStruct((tokens, features), BF16)
    hot_emb, pick, signal, back = pl.pallas_call(
        functools.partial(own_kernel, shard_rows, 1.0 / math.sqrt(bal * tokens)),
        out_shape=(wide, jax.ShapeDtypeStruct((tokens, tokens), BF16), wide, wide),
        in_specs=[smem] + [vmem] * 5,
        out_specs=(vmem,) * 4,
        name="own",
    )(hist_lengths, item_ids.reshape(1, tokens), hot_table, hot_rows, out_grad, w_out)

    width = (hidden + features) // 2
    piece = jax.ShapeDtypeStruct((bal // 2, features // bal, width), BF16)
    layer_out, a_send, a_keep, b_send, b_keep = pl.pallas_call(
        layer_kernel,
        out_shape=(wide,) + (piece,) * 4,
        in_specs=[smem] + [vmem] * 7,
        out_specs=(vmem,) * 5,
        scratch_shapes=[
            pltpu.VMEM((features, tokens), BF16),
            pltpu.VMEM((features, tokens), BF16),
            pltpu.VMEM((tokens, hidden), BF16),
            pltpu.VMEM((tokens, features), BF16),
            pltpu.VMEM((tokens, hidden), F32),
        ],
        name="layer",
    )(hist_lengths, hot_emb, pick, replies, signal, back, w_uvqk, w_out)

    first_order, second_order = bit_orders(bal)
    a = halve(a_send, a_keep, first_order, bal)
    b = halve(b_send, b_keep, second_order, bal)
    grad_first = jnp.concatenate([a, b[:, : hidden - width]], axis=1)
    return (layer_out, grad_first, b[:, hidden - width :])


def solution(mesh):
    return jax.shard_map(
        per_device,
        mesh=mesh,
        in_specs=(
            P(("table", "bal")),
            P(),
            P(),
            P("table", None),
            P(),
            P(("table", "bal"), None),
            P(),
            P(),
        ),
        out_specs=(P(("table", "bal"), None), P(("table", "bal"), None), P(("table", "bal"), None)),
        check_vma=False,
    )
```

time: 193 us -> 67.7 us (0.35)
  waiting for transfers between devices: 90.3 us -> 25.2 us
  local copies, waits for them, and re-layouts: 27 us -> 2.23 us
  other arithmetic: 23.4 us -> 2.6 us
  matrix products: 20.4 us -> 0 us
  Pallas kernels: 0 us -> 15.2 us
  between operations: 14.2 us -> 0.68 us
  starting transfers between devices: 3.67 us -> 9.55 us
  loops' own time: 2 us -> 0 us
    reduce_scatter x2 -> x0, waiting for transfers between devices: 81.5 us -> none  [the longest x1 56.2 us: per_device(): lax.psum_scatter(totals[0], 'bal', scatter_dimension=0, tiled=True)]
    dot_general x22 -> x0, matrix products: 20.4 us -> none  [the longest x2 8.14 us: user_pass(): jnp.einsum('td,tf->df', normed, grad_hidden, preferred_element_type=jnp.f...]
    ppermute x0 -> x4, waiting for transfers between devices: none -> 18.9 us  [halve(): got = lax.ppermute(send, 'bal', [(i, i ^ bit) for i in range(count)])]
    pallas_call x0 -> x3, Pallas kernels: none -> 15.2 us  [the longest x1 8.92 us: per_device(): pl.pallas_call(layer_kernel, out_shape=(wide,) + (piece,) * 4, in_specs=[...]
    add x4 -> x2, other arithmetic: 12.8 us -> 1.41 us  [halve(): total = got.astype(F32) + keep.astype(F32)]
    scatter x1 -> x0, local copies, waits for them, and re-layouts: 11.2 us -> none  [per_device(): jnp.zeros((owners, capacity), jnp.int32).at[target, position]]
    gather x4 -> x0, local copies, waits for them, and re-layouts: 6.4 us -> none  [the longest x1 2.09 us: per_device(): cold_part = replies[owner_of, jnp.minimum(position, capacity - 1)]]
    ppermute x0 -> x4, starting transfers between devices: none -> 6.14 us  [halve(): got = lax.ppermute(send, 'bal', [(i, i ^ bit) for i in range(count)])]
  transfers between devices with their start and end apart: 3 -> 5, of which waited for: 3 -> 4; matrix products, arithmetic and copies ran while one was open for 1% -> 3% of each run, Pallas kernels for 0% -> 5%
where the time goes in v1:
time: 67.7 us; the launch traced here: 67.3 us
  waiting for transfers between devices  25.2 us (37%)
  Pallas kernels  15.2 us (22%)
  blocking collectives  11.9 us (18%)
  starting transfers between devices  9.55 us (14%)
  other arithmetic  2.6 us (4%)
  local copies, waits for them, and re-layouts  2.23 us (3%)
  between operations  0.68 us (1%)
    ppermute x4, waiting for transfers between devices, halve(): got = lax.ppermute(send, 'bal', [(i, i ^ bit) for i in range(count)])  18.9 us
    all_to_all x1, blocking collectives, per_device(): lax.all_to_all(everyone, 'table', split_axis=0, concat_axis=0, tiled=True)  11.9 us
    pallas_call x1, Pallas kernels, per_device(): pl.pallas_call(layer_kernel, out_shape=(wide,) + (piece,) * 4, in_specs=[...  8.92 us
    all_to_all x1, waiting for transfers between devices, per_device(): lax.all_to_all(found, 'table', split_axis=0, concat_axis=0, tiled=True)  6.28 us
    ppermute x4, starting transfers between devices, halve(): got = lax.ppermute(send, 'bal', [(i, i ^ bit) for i in range(count)])  6.14 us
    all_to_all x1, starting transfers between devices, per_device(): lax.all_to_all(found, 'table', split_axis=0, concat_axis=0, tiled=True)  3.41 us
    pallas_call x1, Pallas kernels, per_device(): pl.pallas_call(functools.partial(own_kernel, shard_rows, 1.0 / math.sqrt(...  3.35 us
    pallas_call x1, Pallas kernels, per_device(): pl.pallas_call(functools.partial(serve_kernel, hot_count), out_shape=jax....  2.94 us
  transfers between devices with their start and end apart: 5, of which 4 were waited for; matrix products, arithmetic and copies ran while one was open for 3% of the time, Pallas kernels for 5%

profile of v1, /device:TPU:0, one launch (start us, length us, event | category | flops | bytes accessed | tf_op | source)
XLA Modules:
  0.0 67.3 jit_solution(15333563191531866714)
XLA Ops:
  0.6 0.7 %broadcast_in_dim.2 = s32[8,1,256]{2,1,0:T(1,128)S(1)} broadcast(s32[256]{0:T(256)} %param.8), dimensions={2} | broadcast | bytes 9216 | tf_op jit(solution)/shard_map/broadcast_in_dim | solution.py:253
  1.3 11.9 %all_to_all.16.ids_ref = s32[8,1,256]{2,1,0:T(1,128)} all-to-all(s32[8,1,256]{2,1,0:T(1,128)S(1)} %broadcast_in_dim.2), channel_id=1, replica_groups=mesh['table'=8,'bal'=4] {'table'}, dimensions={0} | all-to-all | bytes 16384 | tf_op jit(solution)/shard_map/all_to_all | solution.py:254
  13.2 2.9 %serve.1 = bf16[256,512]{1,0:T(8,128)(2,1)} custom-call(s32[8,1,256]{2,1,0:T(1,128)} %all_to_all.16.ids_ref, s32[64,128]{1,0:T(8,128)} %bitcast.10, bf16[1024,512]{1,0:T(8,128)(2,1)} %cold_ref.1), custom_call_target="tpu_custom_call" | custom-call | tf_op jit(solution)/shard_map/serve/pallas_call | solution.py:255
  16.1 3.4 %all-to-all-start.1 = ((bf16[8,32,512]{2,1,0:T(8,128)(2,1)}), bf16[8,32,512]{2,1,0:T(8,128)(2,1)S(1)}, u32[]{:S(2)}, u32[]{:S(2)}) async-start(bf16[8,32,512]{2,1,0:T(8,128)(2,1)} %bitcast.9), calls=%async_computation.1 | async-start | bytes 524288 | tf_op jit(solution)/shard_map/all_to_all | solution.py:262
  19.5 3.4 %own.1 = (bf16[256,512]{1,0:T(8,128)(2,1)}, bf16[256,256]{1,0:T(8,128)(2,1)}, bf16[256,512]{1,0:T(8,128)(2,1)}, bf16[256,512]{1,0:T(8,128)(2,1)}) custom-call(s32[64]{0:T(128)} %len_ref.3, s32[1,256]{1,0:T(1,128)} %bitcast.12, s32[64,128]{1,0:T(8,128)} %bitcast.11, bf16[1024,512]{1,0:T(8,128)(2,1)} %hot_rows_ref.1, bf16[256,512]{1,0:T(8,128)(2,1)} %cot_ref.1, ...), custom_call_target="tpu_custom_call" | custom-call | tf_op jit(solution)/shard_map/own/pallas_call | solution.py:265
  22.9 6.3 %all-to-all-done.1 = bf16[8,32,512]{2,1,0:T(8,128)(2,1)S(1)} async-done(((bf16[8,32,512]{2,1,0:T(8,128)(2,1)}), bf16[8,32,512]{2,1,0:T(8,128)(2,1)S(1)}, u32[]{:S(2)}, u32[]{:S(2)}) %all-to-all-start.1) | async-done | bytes 262176 | tf_op jit(solution)/shard_map/all_to_all | solution.py:262
  29.2 0.0 copy-start
  29.2 0.7 %copy-done = bf16[8,32,512]{2,1,0:T(8,128)(2,1)} copy-done((bf16[8,32,512]{2,1,0:T(8,128)(2,1)}, bf16[8,32,512]{2,1,0:T(8,128)(2,1)S(1)}, u32[]{:S(2)}) %copy-start) | copy-done | bytes 262168
  29.9 8.9 %layer.1 = (bf16[256,512]{1,0:T(8,128)(2,1)}, bf16[2,128,1280]{2,1,0:T(8,128)(2,1)}, bf16[2,128,1280]{2,1,0:T(8,128)(2,1)}, bf16[2,128,1280]{2,1,0:T(8,128)(2,1)}, bf16[2,128,1280]{2,1,0:T(8,128)(2,1)}) custom-call(s32[64]{0:T(128)} %len_ref.3, bf16[256,512]{1,0:T(8,128)(2,1)} %get-tuple-element.12.emb_ref, bf16[256,256]{1,0:T(8,128)(2,1)} %get-tuple-element.13.pick_ref, ...), custom_call_target="tpu_custom_call" | custom-call | tf_op jit(solution)/shard_map/layer/pallas_call | solution.py:275
  38.8 1.5 %collective-permute-start.2 = (bf16[2,128,1280]{2,1,0:T(8,128)(2,1)}, bf16[2,128,1280]{2,1,0:T(8,128)(2,1)S(1)}, u32[]{:S(2)}, u32[]{:S(2)}) collective-permute-start(bf16[2,128,1280]{2,1,0:T(8,128)(2,1)} %get-tuple-element.19), channel_id=1, source_target_pairs={{0,2},{1,3},{2,0},{3,1},{4,6},{5,7},{6,4},{7,5},{8,10},{9,11},{10,... | collective-permute-start | bytes 1966088 | tf_op jit(solution)/shard_map/ppermute | solution.py:230
  40.3 1.5 %collective-permute-start = (bf16[2,128,1280]{2,1,0:T(8,128)(2,1)}, bf16[2,128,1280]{2,1,0:T(8,128)(2,1)S(1)}, u32[]{:S(2)}, u32[]{:S(2)}) collective-permute-start(bf16[2,128,1280]{2,1,0:T(8,128)(2,1)} %get-tuple-element.17), channel_id=1, source_target_pairs={{0,1},{1,0},{2,3},{3,2},{4,5},{5,4},{6,7},{7,6},{8,9},{9,8},{10,11... | collective-permute-start | bytes 1966088 | tf_op jit(solution)/shard_map/ppermute | solution.py:230
  41.8 13.3 %collective-permute-done.2 = bf16[2,128,1280]{2,1,0:T(8,128)(2,1)S(1)} collective-permute-done((bf16[2,128,1280]{2,1,0:T(8,128)(2,1)}, bf16[2,128,1280]{2,1,0:T(8,128)(2,1)S(1)}, u32[]{:S(2)}, u32[]{:S(2)}) %collective-permute-start.2) | collective-permute-done | bytes 655392 | tf_op jit(solution)/shard_map/ppermute | solution.py:230
  55.1 0.0 copy-start.1
  55.1 1.3 %convert_add_fusion = f32[2,128,1280]{2,1,0:T(8,128)S(1)} fusion(bf16[2,128,1280]{2,1,0:T(8,128)(2,1)} %get-tuple-element.20, bf16[2,128,1280]{2,1,0:T(8,128)(2,1)S(1)} %collective-permute-done.2), kind=kLoop, calls=%fused_computation | loop fusion | flops 983040 | bytes 2621440 | tf_op jit(solution)/shard_map/add | solution.py:231
  56.4 1.6 %collective-permute-start.3 = (bf16[1,128,1280]{2,1,0:T(8,128)(2,1)S(1)}, bf16[1,128,1280]{2,1,0:T(8,128)(2,1)S(1)}, u32[]{:S(2)}, u32[]{:S(2)}) collective-permute-start(bf16[1,128,1280]{2,1,0:T(8,128)(2,1)S(1)} %slice.40), channel_id=1, source_target_pairs={{0,1},{1,0},{2,3},{3,2},{4,5},{5,4},{6,7},{7,6},{8,9},{9,8},{10,11... | collective-permute-start | bytes 983048 | tf_op jit(solution)/shard_map/ppermute | solution.py:230
  58.0 0.0 collective-permute-done
  58.0 0.0 copy-done.1
  58.0 0.1 convert_add_fusion.1
  58.2 1.6 %collective-permute-start.1 = (bf16[1,128,1280]{2,1,0:T(8,128)(2,1)S(1)}, bf16[1,128,1280]{2,1,0:T(8,128)(2,1)S(1)}, u32[]{:S(2)}, u32[]{:S(2)}) collective-permute-start(bf16[1,128,1280]{2,1,0:T(8,128)(2,1)S(1)} %slice.41), channel_id=1, source_target_pairs={{0,2},{1,3},{2,0},{3,1},{4,6},{5,7},{6,4},{7,5},{8,10},{9,11},{10,... | collective-permute-start | bytes 983048 | tf_op jit(solution)/shard_map/ppermute | solution.py:230
  59.8 5.0 %collective-permute-done.3 = bf16[1,128,1280]{2,1,0:T(8,128)(2,1)S(1)} collective-permute-done((bf16[1,128,1280]{2,1,0:T(8,128)(2,1)S(1)}, bf16[1,128,1280]{2,1,0:T(8,128)(2,1)S(1)}, u32[]{:S(2)}, u32[]{:S(2)}) %collective-permute-start.3) | collective-permute-done | bytes 327712 | tf_op jit(solution)/shard_map/ppermute | solution.py:230
  64.7 0.1 fusion
  64.8 0.7 %slice.31 = f32[128,512]{1,0:T(8,128)} slice(f32[128,1280]{1,0:T(8,128)S(1)} %fusion), slice={[0:128], [768:1280]} | slice | bytes 524288 | tf_op jit(solution)/shard_map/slice | solution.py:294
  65.5 0.7 collective-permute-done.1
  66.2 0.1 fusion.1
  66.2 1.1 %pad_maximum_fusion = f32[128,2048]{1,0:T(8,128)} fusion(f32[128,768]{1,0:T(8,128)S(1)} %slice.30, f32[128,1280]{1,0:T(8,128)S(1)} %fusion.1), kind=kLoop, calls=%fused_computation.2 | loop fusion | flops 262144 | bytes 2097152 | tf_op jit(solution)/shard_map/concatenate | solution.py:293
  (3 shorter events, 0.1 us)
Async XLA Ops:
  16.1 13.1 %all-to-all-start.1 = ((bf16[8,32,512]{2,1,0:T(8,128)(2,1)}), bf16[8,32,512]{2,1,0:T(8,128)(2,1)S(1)}, u32[]{:S(2)}, u32[]{:S(2)}) async-start(bf16[8,32,512]{2,1,0:T(8,128)(2,1)} %bitcast.9), calls=%async_computation.1 | async-start | bytes 524288 | tf_op jit(solution)/shard_map/all_to_all | solution.py:262
  29.2 0.7 %copy-start = (bf16[8,32,512]{2,1,0:T(8,128)(2,1)}, bf16[8,32,512]{2,1,0:T(8,128)(2,1)S(1)}, u32[]{:S(2)}) copy-start(bf16[8,32,512]{2,1,0:T(8,128)(2,1)S(1)} %all-to-all-done.1) | copy-start | bytes 786436
  38.8 16.3 %collective-permute-start.2 = (bf16[2,128,1280]{2,1,0:T(8,128)(2,1)}, bf16[2,128,1280]{2,1,0:T(8,128)(2,1)S(1)}, u32[]{:S(2)}, u32[]{:S(2)}) collective-permute-start(bf16[2,128,1280]{2,1,0:T(8,128)(2,1)} %get-tuple-element.19), channel_id=1, source_target_pairs={{0,2},{1,3},{2,0},{3,1},{4,6},{5,7},{6,4},{7,5},{8,10},{9,11},{10,... | collective-permute-start | bytes 1966088 | tf_op jit(solution)/shard_map/ppermute | solution.py:230
  40.3 17.7 %collective-permute-start = (bf16[2,128,1280]{2,1,0:T(8,128)(2,1)}, bf16[2,128,1280]{2,1,0:T(8,128)(2,1)S(1)}, u32[]{:S(2)}, u32[]{:S(2)}) collective-permute-start(bf16[2,128,1280]{2,1,0:T(8,128)(2,1)} %get-tuple-element.17), channel_id=1, source_target_pairs={{0,1},{1,0},{2,3},{3,2},{4,5},{5,4},{6,7},{7,6},{8,9},{9,8},{10,11... | collective-permute-start | bytes 1966088 | tf_op jit(solution)/shard_map/ppermute | solution.py:230
  55.1 2.9 %copy-start.1 = (bf16[2,128,1280]{2,1,0:T(8,128)(2,1)S(1)}, bf16[2,128,1280]{2,1,0:T(8,128)(2,1)}, u32[]{:S(2)}) copy-start(bf16[2,128,1280]{2,1,0:T(8,128)(2,1)} %get-tuple-element.18) | copy-start | bytes 1966084
  56.4 8.3 %collective-permute-start.3 = (bf16[1,128,1280]{2,1,0:T(8,128)(2,1)S(1)}, bf16[1,128,1280]{2,1,0:T(8,128)(2,1)S(1)}, u32[]{:S(2)}, u32[]{:S(2)}) collective-permute-start(bf16[1,128,1280]{2,1,0:T(8,128)(2,1)S(1)} %slice.40), channel_id=1, source_target_pairs={{0,1},{1,0},{2,3},{3,2},{4,5},{5,4},{6,7},{7,6},{8,9},{9,8},{10,11... | collective-permute-start | bytes 983048 | tf_op jit(solution)/shard_map/ppermute | solution.py:230
  58.2 8.0 %collective-permute-start.1 = (bf16[1,128,1280]{2,1,0:T(8,128)(2,1)S(1)}, bf16[1,128,1280]{2,1,0:T(8,128)(2,1)S(1)}, u32[]{:S(2)}, u32[]{:S(2)}) collective-permute-start(bf16[1,128,1280]{2,1,0:T(8,128)(2,1)S(1)} %slice.41), channel_id=1, source_target_pairs={{0,2},{1,3},{2,0},{3,1},{4,6},{5,7},{6,4},{7,5},{8,10},{9,11},{10,... | collective-permute-start | bytes 983048 | tf_op jit(solution)/shard_map/ppermute | solution.py:230

commit v2 on v1

--- a/solution.py
+++ b/solution.py
@@ -11,6 +11,9 @@
 HEADS = 4
 MAXLEN = 128
 LANES = 128
+VM_SERVE = 8 << 20
+VM_OWN = 8 << 20
+VM_LAYER = 20 << 20
 F32 = jnp.float32
 BF16 = jnp.bfloat16
 
@@ -257,6 +260,7 @@
         out_shape=jax.ShapeDtypeStruct((tokens, features), BF16),
         in_specs=[vmem] * 3,
         out_specs=vmem,
+        compiler_params=pltpu.CompilerParams(vmem_limit_bytes=VM_SERVE),
         name="serve",
     )(asked, hot_table, cold_rows)
     replies = lax.all_to_all(found, "table", split_axis=0, concat_axis=0, tiled=True)
@@ -267,6 +271,7 @@
         out_shape=(wide, jax.ShapeDtypeStruct((tokens, tokens), BF16), wide, wide),
         in_specs=[smem] + [vmem] * 5,
         out_specs=(vmem,) * 4,
+        compiler_params=pltpu.CompilerParams(vmem_limit_bytes=VM_OWN),
         name="own",
     )(hist_lengths, item_ids.reshape(1, tokens), hot_table, hot_rows, out_grad, w_out)
 
@@ -284,6 +289,7 @@
             pltpu.VMEM((tokens, features), BF16),
             pltpu.VMEM((tokens, hidden), F32),
         ],
+        compiler_params=pltpu.CompilerParams(vmem_limit_bytes=VM_LAYER),
         name="layer",
     )(hist_lengths, hot_emb, pick, replies, signal, back, w_uvqk, w_out)
 

time: 67.7 us -> 65.2 us (0.963)
  local copies, waits for them, and re-layouts: 2.23 us -> 8.15 us
  Pallas kernels: 15.2 us -> 9.87 us
  waiting for transfers between devices: 25.2 us -> 23 us
  other arithmetic: 2.6 us -> 1.48 us
    unnamed x4 -> x22, local copies, waits for them, and re-layouts: 0.71 us -> 6.57 us
    pallas_call x1, Pallas kernels: 8.92 us -> 6.49 us  [per_device(): pl.pallas_call(layer_kernel, out_shape=(wide,) + (piece,) * 4, in_specs=[...]
    all_to_all x1, waiting for transfers between devices: 6.28 us -> 4.27 us  [per_device(): lax.all_to_all(found, 'table', split_axis=0, concat_axis=0, tiled=True)]
    pallas_call x1, Pallas kernels: 3.35 us -> 1.69 us  [per_device(): pl.pallas_call(functools.partial(own_kernel, shard_rows, 1.0 / math.sqrt(...]
    pallas_call x1, Pallas kernels: 2.94 us -> 1.69 us  [per_device(): pl.pallas_call(functools.partial(serve_kernel, hot_count), out_shape=jax....]
    add x2, other arithmetic: 1.41 us -> 0.29 us  [halve(): total = got.astype(F32) + keep.astype(F32)]
  transfers between devices with their start and end apart: 5 -> 5, of which waited for: 4 -> 4; matrix products, arithmetic and copies ran while one was open for 3% -> 2% of each run, Pallas kernels for 5% -> 3%
where the time goes in v2:
time: 65.2 us; the launch traced here: 64.7 us
  waiting for transfers between devices  23 us (35%)
  blocking collectives  11.7 us (18%)
  Pallas kernels  9.87 us (15%)
  starting transfers between devices  9.69 us (15%)
  local copies, waits for them, and re-layouts  8.15 us (12%)
  other arithmetic  1.48 us (2%)
  between operations  0.74 us (1%)
    ppermute x4, waiting for transfers between devices, halve(): got = lax.ppermute(send, 'bal', [(i, i ^ bit) for i in range(count)])  18.7 us
    all_to_all x1, blocking collectives, per_device(): lax.all_to_all(everyone, 'table', split_axis=0, concat_axis=0, tiled=True)  11.7 us
    unnamed x22, local copies, waits for them, and re-layouts  6.57 us
    pallas_call x1, Pallas kernels, per_device(): pl.pallas_call(layer_kernel, out_shape=(wide,) + (piece,) * 4, in_specs=[...  6.49 us
    ppermute x4, starting transfers between devices, halve(): got = lax.ppermute(send, 'bal', [(i, i ^ bit) for i in range(count)])  6.15 us
    all_to_all x1, waiting for transfers between devices, per_device(): lax.all_to_all(found, 'table', split_axis=0, concat_axis=0, tiled=True)  4.27 us
    all_to_all x1, starting transfers between devices, per_device(): lax.all_to_all(found, 'table', split_axis=0, concat_axis=0, tiled=True)  3.54 us
    pallas_call x1, Pallas kernels, per_device(): pl.pallas_call(functools.partial(serve_kernel, hot_count), out_shape=jax....  1.69 us
  transfers between devices with their start and end apart: 5, of which 4 were waited for; matrix products, arithmetic and copies ran while one was open for 2% of the time, Pallas kernels for 3%

profile of v2, /device:TPU:0, one launch (start us, length us, event | category | flops | bytes accessed | tf_op | source)
XLA Modules:
  0.0 64.7 jit_solution(15644367518023219609)
XLA Ops:
  0.6 0.0 copy-start.1
  0.6 0.7 %broadcast_in_dim.2 = s32[8,1,256]{2,1,0:T(1,128)S(1)} broadcast(s32[256]{0:T(256)} %param.8), dimensions={2} | broadcast | bytes 9216 | tf_op jit(solution)/shard_map/broadcast_in_dim | solution.py:256
  1.4 11.7 %all_to_all.16.ids_ref = s32[8,1,256]{2,1,0:T(1,128)S(1)} all-to-all(s32[8,1,256]{2,1,0:T(1,128)S(1)} %broadcast_in_dim.2), channel_id=1, replica_groups=mesh['table'=8,'bal'=4] {'table'}, dimensions={0} | all-to-all | bytes 16384 | tf_op jit(solution)/shard_map/all_to_all | solution.py:257
  13.1 1.2 %copy-done.2 = bf16[1024,512]{1,0:T(8,128)(2,1)S(1)} copy-done((bf16[1024,512]{1,0:T(8,128)(2,1)S(1)}, bf16[1024,512]{1,0:T(8,128)(2,1)}, u32[]{:S(2)}) %copy-start.2) | copy-done | bytes 1048600
  14.4 0.8 %copy-done.7 = s32[8192]{0:T(1024)S(1)} copy-done((s32[8192]{0:T(1024)S(1)}, s32[8192]{0:T(1024)}, u32[]{:S(2)}) %copy-start.7) | copy-done | bytes 32792
  15.1 1.7 %serve.1 = bf16[256,512]{1,0:T(8,128)(2,1)} custom-call(s32[8,1,256]{2,1,0:T(1,128)S(1)} %all_to_all.16.ids_ref, s32[64,128]{1,0:T(8,128)S(1)} %bitcast.9, bf16[1024,512]{1,0:T(8,128)(2,1)S(1)} %copy-done.2), custom_call_target="tpu_custom_call" | custom-call | tf_op jit(solution)/shard_map/serve/pallas_call | solution.py:258
  16.8 3.5 %all-to-all-start.1 = ((bf16[8,32,512]{2,1,0:T(8,128)(2,1)}), bf16[8,32,512]{2,1,0:T(8,128)(2,1)S(1)}, u32[]{:S(2)}, u32[]{:S(2)}) async-start(bf16[8,32,512]{2,1,0:T(8,128)(2,1)} %bitcast.2), calls=%async_computation.1 | async-start | bytes 524288 | tf_op jit(solution)/shard_map/all_to_all | solution.py:266
  20.4 0.0 copy-done.1
  20.4 0.0 copy-start.3
  20.4 1.2 %copy-done.3 = bf16[1024,512]{1,0:T(8,128)(2,1)S(1)} copy-done((bf16[1024,512]{1,0:T(8,128)(2,1)S(1)}, bf16[1024,512]{1,0:T(8,128)(2,1)}, u32[]{:S(2)}) %copy-start.3) | copy-done | bytes 1048600
  21.6 0.9 %copy-done.6 = bf16[256,512]{1,0:T(8,128)(2,1)S(1)} copy-done((bf16[256,512]{1,0:T(8,128)(2,1)S(1)}, bf16[256,512]{1,0:T(8,128)(2,1)}, u32[]{:S(2)}) %copy-start.6) | copy-done | bytes 262168
  22.6 0.8 %copy-done.8 = s32[8192]{0:T(1024)S(1)} copy-done((s32[8192]{0:T(1024)S(1)}, s32[8192]{0:T(1024)}, u32[]{:S(2)}) %copy-start.8) | copy-done | bytes 32792
  23.3 1.7 %own.1 = (bf16[256,512]{1,0:T(8,128)(2,1)S(1)}, bf16[256,256]{1,0:T(8,128)(2,1)S(1)}, bf16[256,512]{1,0:T(8,128)(2,1)S(1)}, bf16[256,512]{1,0:T(8,128)(2,1)S(1)}) custom-call(s32[64]{0:T(128)S(1)} %copy-done.10, s32[1,256]{1,0:T(1,128)S(1)} %bitcast.11, s32[64,128]{1,0:T(8,128)S(1)} %bitcast.10, bf16[1024,512]{1,0:T(8,128)(2,1)S(1)} %copy-done.3, ...), custom_call_target="tpu_custom_call" | custom-call | tf_op jit(solution)/shard_map/own/pallas_call | solution.py:269
  25.0 0.0 copy-start.4
  25.0 0.7 %copy-done.4 = bf16[256,512]{1,0:T(8,128)(2,1)} copy-done((bf16[256,512]{1,0:T(8,128)(2,1)}, bf16[256,512]{1,0:T(8,128)(2,1)S(1)}, u32[]{:S(2)}) %copy-start.4) | copy-done | bytes 262168
  25.7 4.3 %all-to-all-done.1 = bf16[8,32,512]{2,1,0:T(8,128)(2,1)S(1)} async-done(((bf16[8,32,512]{2,1,0:T(8,128)(2,1)}), bf16[8,32,512]{2,1,0:T(8,128)(2,1)S(1)}, u32[]{:S(2)}, u32[]{:S(2)}) %all-to-all-start.1) | async-done | bytes 262176 | tf_op jit(solution)/shard_map/all_to_all | solution.py:266
  30.0 0.9 %copy-done.5 = bf16[256,512]{1,0:T(8,128)(2,1)S(1)} copy-done((bf16[256,512]{1,0:T(8,128)(2,1)S(1)}, bf16[256,512]{1,0:T(8,128)(2,1)}, u32[]{:S(2)}) %copy-start.5) | copy-done | bytes 262168
  31.0 6.5 %layer.1 = (bf16[256,512]{1,0:T(8,128)(2,1)}, bf16[2,128,1280]{2,1,0:T(8,128)(2,1)S(1)}, bf16[2,128,1280]{2,1,0:T(8,128)(2,1)S(1)}, bf16[2,128,1280]{2,1,0:T(8,128)(2,1)S(1)}, bf16[2,128,1280]{2,1,0:T(8,128)(2,1)S(1)}) custom-call(s32[64]{0:T(128)S(1)} %copy-done.10, bf16[256,512]{1,0:T(8,128)(2,1)S(1)} %get-tuple-element.12.emb_ref, ...), custom_call_target="tpu_custom_call" | custom-call | tf_op jit(solution)/shard_map/layer/pallas_call | solution.py:280
  37.5 1.5 %collective-permute-start.2 = (bf16[2,128,1280]{2,1,0:T(8,128)(2,1)S(1)}, bf16[2,128,1280]{2,1,0:T(8,128)(2,1)S(1)}, u32[]{:S(2)}, u32[]{:S(2)}) collective-permute-start(bf16[2,128,1280]{2,1,0:T(8,128)(2,1)S(1)} %get-tuple-element.19), channel_id=1, source_target_pairs={{0,2},{1,3},{2,0},{3,1},{4,6},{5,7},{6,4},{7,5},{8,10},{9,11},{10,... | collective-permute-start | bytes 1966088 | tf_op jit(solution)/shard_map/ppermute | solution.py:233
  39.0 1.5 %collective-permute-start = (bf16[2,128,1280]{2,1,0:T(8,128)(2,1)S(1)}, bf16[2,128,1280]{2,1,0:T(8,128)(2,1)S(1)}, u32[]{:S(2)}, u32[]{:S(2)}) collective-permute-start(bf16[2,128,1280]{2,1,0:T(8,128)(2,1)S(1)} %get-tuple-element.17), channel_id=1, source_target_pairs={{0,1},{1,0},{2,3},{3,2},{4,5},{5,4},{6,7},{7,6},{8,9},{9,8},{10,11... | collective-permute-start | bytes 1966088 | tf_op jit(solution)/shard_map/ppermute | solution.py:233
  40.5 13.1 %collective-permute-done.2 = bf16[2,128,1280]{2,1,0:T(8,128)(2,1)S(1)} collective-permute-done((bf16[2,128,1280]{2,1,0:T(8,128)(2,1)S(1)}, bf16[2,128,1280]{2,1,0:T(8,128)(2,1)S(1)}, u32[]{:S(2)}, u32[]{:S(2)}) %collective-permute-start.2) | collective-permute-done | bytes 655392 | tf_op jit(solution)/shard_map/ppermute | solution.py:233
  53.6 0.1 convert_add_fusion
  53.7 1.6 %collective-permute-start.3 = (bf16[1,128,1280]{2,1,0:T(8,128)(2,1)S(1)}, bf16[1,128,1280]{2,1,0:T(8,128)(2,1)S(1)}, u32[]{:S(2)}, u32[]{:S(2)}) collective-permute-start(bf16[1,128,1280]{2,1,0:T(8,128)(2,1)S(1)} %slice.40), channel_id=1, source_target_pairs={{0,1},{1,0},{2,3},{3,2},{4,5},{5,4},{6,7},{7,6},{8,9},{9,8},{10,11... | collective-permute-start | bytes 983048 | tf_op jit(solution)/shard_map/ppermute | solution.py:233
  55.3 0.0 collective-permute-done
  55.3 0.2 convert_add_fusion.1
  55.5 1.6 %collective-permute-start.1 = (bf16[1,128,1280]{2,1,0:T(8,128)(2,1)S(1)}, bf16[1,128,1280]{2,1,0:T(8,128)(2,1)S(1)}, u32[]{:S(2)}, u32[]{:S(2)}) collective-permute-start(bf16[1,128,1280]{2,1,0:T(8,128)(2,1)S(1)} %slice.41), channel_id=1, source_target_pairs={{0,2},{1,3},{2,0},{3,1},{4,6},{5,7},{6,4},{7,5},{8,10},{9,11},{10,... | collective-permute-start | bytes 983048 | tf_op jit(solution)/shard_map/ppermute | solution.py:233
  57.1 5.0 %collective-permute-done.3 = bf16[1,128,1280]{2,1,0:T(8,128)(2,1)S(1)} collective-permute-done((bf16[1,128,1280]{2,1,0:T(8,128)(2,1)S(1)}, bf16[1,128,1280]{2,1,0:T(8,128)(2,1)S(1)}, u32[]{:S(2)}, u32[]{:S(2)}) %collective-permute-start.3) | collective-permute-done | bytes 327712 | tf_op jit(solution)/shard_map/ppermute | solution.py:233
  62.0 0.1 fusion
  62.1 0.7 %slice.31 = f32[128,512]{1,0:T(8,128)} slice(f32[128,1280]{1,0:T(8,128)S(1)} %fusion), slice={[0:128], [768:1280]} | slice | bytes 524288 | tf_op jit(solution)/shard_map/slice | solution.py:300
  62.9 0.7 %collective-permute-done.1 = bf16[1,128,1280]{2,1,0:T(8,128)(2,1)S(1)} collective-permute-done((bf16[1,128,1280]{2,1,0:T(8,128)(2,1)S(1)}, bf16[1,128,1280]{2,1,0:T(8,128)(2,1)S(1)}, u32[]{:S(2)}, u32[]{:S(2)}) %collective-permute-start.1) | collective-permute-done | bytes 327712 | tf_op jit(solution)/shard_map/ppermute | solution.py:233
  63.5 0.1 fusion.1
  63.6 1.1 %pad_maximum_fusion = f32[128,2048]{1,0:T(8,128)} fusion(f32[128,768]{1,0:T(8,128)S(1)} %slice.30, f32[128,1280]{1,0:T(8,128)S(1)} %fusion.1), kind=kLoop, calls=%fused_computation.2 | loop fusion | flops 262144 | bytes 2097152 | tf_op jit(solution)/shard_map/concatenate | solution.py:299
  (14 shorter events, 0.1 us)
Async XLA Ops:
  0.6 19.7 %copy-start.1 = (bf16[512,512]{1,0:T(8,128)(2,1)S(1)}, bf16[512,512]{1,0:T(8,128)(2,1)}, u32[]{:S(2)}) copy-start(bf16[512,512]{1,0:T(8,128)(2,1)} %w_out_ref.3) | copy-start | bytes 1572868
  13.1 1.2 %copy-start.2 = (bf16[1024,512]{1,0:T(8,128)(2,1)S(1)}, bf16[1024,512]{1,0:T(8,128)(2,1)}, u32[]{:S(2)}) copy-start(bf16[1024,512]{1,0:T(8,128)(2,1)} %cold_ref.1) | copy-start | bytes 3145732
  14.4 0.8 %copy-start.7 = (s32[8192]{0:T(1024)S(1)}, s32[8192]{0:T(1024)}, u32[]{:S(2)}) copy-start(s32[8192]{0:T(1024)} %param.9) | copy-start | bytes 98308
  15.1 5.3 %copy-start.9 = (s32[256]{0:T(256)S(1)}, s32[256]{0:T(256)}, u32[]{:S(2)}) copy-start(s32[256]{0:T(256)} %param.8) | copy-start | bytes 3076
  15.1 5.3 %copy-start.10 = (s32[64]{0:T(128)S(1)}, s32[64]{0:T(128)}, u32[]{:S(2)}) copy-start(s32[64]{0:T(128)} %len_ref.3) | copy-start | bytes 772
  16.8 13.2 %copy-start = (bf16[512,2048]{1,0:T(8,128)(2,1)S(1)}, bf16[512,2048]{1,0:T(8,128)(2,1)}, u32[]{:S(2)}) copy-start(bf16[512,2048]{1,0:T(8,128)(2,1)} %w_ref.1) | copy-start | bytes 6291460
  16.8 13.2 %all-to-all-start.1 = ((bf16[8,32,512]{2,1,0:T(8,128)(2,1)}), bf16[8,32,512]{2,1,0:T(8,128)(2,1)S(1)}, u32[]{:S(2)}, u32[]{:S(2)}) async-start(bf16[8,32,512]{2,1,0:T(8,128)(2,1)} %bitcast.2), calls=%async_computation.1 | async-start | bytes 524288 | tf_op jit(solution)/shard_map/all_to_all | solution.py:266
  20.4 1.2 %copy-start.3 = (bf16[1024,512]{1,0:T(8,128)(2,1)S(1)}, bf16[1024,512]{1,0:T(8,128)(2,1)}, u32[]{:S(2)}) copy-start(bf16[1024,512]{1,0:T(8,128)(2,1)} %hot_rows_ref.1) | copy-start | bytes 3145732
  21.6 0.9 %copy-start.6 = (bf16[256,512]{1,0:T(8,128)(2,1)S(1)}, bf16[256,512]{1,0:T(8,128)(2,1)}, u32[]{:S(2)}) copy-start(bf16[256,512]{1,0:T(8,128)(2,1)} %cot_ref.1) | copy-start | bytes 786436
  22.6 0.8 %copy-start.8 = (s32[8192]{0:T(1024)S(1)}, s32[8192]{0:T(1024)}, u32[]{:S(2)}) copy-start(s32[8192]{0:T(1024)} %param.9) | copy-start | bytes 98308
  25.0 0.7 %copy-start.4 = (bf16[256,512]{1,0:T(8,128)(2,1)}, bf16[256,512]{1,0:T(8,128)(2,1)S(1)}, u32[]{:S(2)}) copy-start(bf16[256,512]{1,0:T(8,128)(2,1)S(1)} %get-tuple-element.15.back_ref) | copy-start | bytes 786436
  30.0 1.0 %copy-start.5 = (bf16[256,512]{1,0:T(8,128)(2,1)S(1)}, bf16[256,512]{1,0:T(8,128)(2,1)}, u32[]{:S(2)}) copy-start(bf16[256,512]{1,0:T(8,128)(2,1)} %copy-done.4) | copy-start | bytes 786436
  37.5 16.1 %collective-permute-start.2 = (bf16[2,128,1280]{2,1,0:T(8,128)(2,1)S(1)}, bf16[2,128,1280]{2,1,0:T(8,128)(2,1)S(1)}, u32[]{:S(2)}, u32[]{:S(2)}) collective-permute-start(bf16[2,128,1280]{2,1,0:T(8,128)(2,1)S(1)} %get-tuple-element.19), channel_id=1, source_target_pairs={{0,2},{1,3},{2,0},{3,1},{4,6},{5,7},{6,4},{7,5},{8,10},{9,11},{10,... | collective-permute-start | bytes 1966088 | tf_op jit(solution)/shard_map/ppermute | solution.py:233
  39.0 16.3 %collective-permute-start = (bf16[2,128,1280]{2,1,0:T(8,128)(2,1)S(1)}, bf16[2,128,1280]{2,1,0:T(8,128)(2,1)S(1)}, u32[]{:S(2)}, u32[]{:S(2)}) collective-permute-start(bf16[2,128,1280]{2,1,0:T(8,128)(2,1)S(1)} %get-tuple-element.17), channel_id=1, source_target_pairs={{0,1},{1,0},{2,3},{3,2},{4,5},{5,4},{6,7},{7,6},{8,9},{9,8},{10,11... | collective-permute-start | bytes 1966088 | tf_op jit(solution)/shard_map/ppermute | solution.py:233
  53.7 8.3 %collective-permute-start.3 = (bf16[1,128,1280]{2,1,0:T(8,128)(2,1)S(1)}, bf16[1,128,1280]{2,1,0:T(8,128)(2,1)S(1)}, u32[]{:S(2)}, u32[]{:S(2)}) collective-permute-start(bf16[1,128,1280]{2,1,0:T(8,128)(2,1)S(1)} %slice.40), channel_id=1, source_target_pairs={{0,1},{1,0},{2,3},{3,2},{4,5},{5,4},{6,7},{7,6},{8,9},{9,8},{10,11... | collective-permute-start | bytes 983048 | tf_op jit(solution)/shard_map/ppermute | solution.py:233
  55.5 8.0 %collective-permute-start.1 = (bf16[1,128,1280]{2,1,0:T(8,128)(2,1)S(1)}, bf16[1,128,1280]{2,1,0:T(8,128)(2,1)S(1)}, u32[]{:S(2)}, u32[]{:S(2)}) collective-permute-start(bf16[1,128,1280]{2,1,0:T(8,128)(2,1)S(1)} %slice.41), channel_id=1, source_target_pairs={{0,2},{1,3},{2,0},{3,1},{4,6},{5,7},{6,4},{7,5},{8,10},{9,11},{10,... | collective-permute-start | bytes 983048 | tf_op jit(solution)/shard_map/ppermute | solution.py:233
